TPU v7x, 512 devices: a whole 4x4x16 slice. The times are simulated.
512 devices in a mesh: aux: 128 (over z, x_hi, y), occ: 4 (over x_lo, core).
Axes of the slice: x: 4 (x_hi: 2, x_lo: 2; x = x_hi * 2 + x_lo), y: 4, z: 16, core: 2. Of those that a mesh axis runs over, the one named last changes fastest.
Arguments:
- integrals: bfloat16 [2304, 32, 6144], P('aux', None, 'occ'), may hold values from -6 to 6
- coefficients: bfloat16 [6144, 48], P('occ'), may hold values from -0.29882812 to 0.29882812
- screening: int32 [32, 48], replicated, may hold values 0 or 1
- metric_factor: bfloat16 [2304, 2304], P('aux'), may hold values from -2 to 4
Outputs:
- gamma_block: bfloat16 [2304, 32, 6144], P('aux', 'occ')
All inputs are finite; a program needn't handle non-finite values.
Results may differ from a plain program's by a relative error of at most 0.0057.
Values may be sent and summed in bfloat16 or wider, within the bound.
A program may use at most 64 MiB of HBM per device.

v0:
```python
import jax
import jax.numpy as jnp
from jax import lax
from jax.sharding import PartitionSpec as P

TILE = 128


def on_device(integrals, coefficients, screening, metric_factor):
    aux_dev, rows_all, basis_part = integrals.shape
    occ_count = coefficients.shape[1]
    occ_size = lax.axis_size("occ")
    occ_index = lax.axis_index("occ")
    rows_dev = rows_all // occ_size
    tiles_part = basis_part // TILE
    screen_tiles = screening.astype(jnp.bfloat16)
    part_tiles = lax.dynamic_slice_in_dim(screen_tiles, occ_index * tiles_part, tiles_part, 1)
    part_screen = jnp.repeat(part_tiles, TILE, axis=1)
    masked = integrals * part_screen[None]
    partial_value = jnp.einsum(
        "pmn,ni->pmi", masked, coefficients, preferred_element_type=jnp.float32
    )
    partial_value = partial_value.reshape(aux_dev, rows_all * occ_count)
    half_transformed = lax.psum_scatter(
        partial_value, "occ", scatter_dimension=1, tiled=True
    ).astype(jnp.bfloat16)
    fitted = jnp.dot(
        metric_factor,
        lax.all_gather(half_transformed, "aux", axis=0, tiled=True),
        preferred_element_type=jnp.float32,
    ).astype(jnp.bfloat16)
    whole_coefficients = lax.all_gather(coefficients, "occ", axis=0, tiled=True)
    own_tiles = lax.dynamic_slice_in_dim(screen_tiles, occ_index * rows_dev, rows_dev, 0)
    own_screen = jnp.repeat(own_tiles, TILE, axis=1).astype(jnp.float32)
    flattened = fitted.reshape(aux_dev * rows_dev, occ_count)
    product = lax.dot_general(
        flattened, whole_coefficients, (((1,), (1,)), ((), ())), preferred_element_type=jnp.float32
    )
    product = product.reshape(aux_dev, rows_dev, whole_coefficients.shape[0])
    return (product * own_screen[None]).astype(jnp.bfloat16)


def solution(mesh):
    return jax.shard_map(
        on_device,
        mesh=mesh,
        in_specs=(P("aux", None, "occ"), P("occ", None), P(), P("aux", None)),
        out_specs=P("aux", "occ", None),
        check_vma=False,
    )
```

profile of v0, /device:TPU:8, one launch (start us, length us, event | category | flops | bytes accessed | tf_op | source)
XLA Modules:
  0.0 273.1 jit_solution(12376429188576232641)
XLA Ops:
  6.5 0.0 copy-start
  6.5 0.0 reduce-scatter.2.cloned.1.call-start
  6.5 0.8 convert_element_type.26
  7.3 0.1 constant_dynamic-slice_fusion
  7.4 0.1 broadcast_in_dim.7
  7.5 0.0 copy-start.1
  7.6 2.1 fusion.1
  9.7 0.8 reshape.15
  10.5 0.0 reduce-scatter.2.cloned.1.call-update
  10.6 0.0 all-gather.3.cloned.1.call-start
  10.6 29.2 %reduce-scatter.2.cloned.1.call-done = f32[18,384]{1,0:T(8,128)} async-done(((f32[18,1536]{1,0:T(8,128)}), f32[18,384]{1,0:T(8,128)}) %reduce-scatter.2.cloned.1.call-update) | async-done | bytes 27664 | tf_op jit(solution)/shard_map/reduce_scatter | solution.py:24
  39.8 1.4 convert_bitcast_fusion
  41.1 0.0 all-gather.3.cloned.1.call-update
  41.2 0.1 copy.7
  41.3 0.0 copy-done.1
  41.3 7.7 %all_gather.7 = bf16[6144,48]{0,1:T(8,128)(2,1)S(1)} all-gather(bf16[1536,48]{0,1:T(8,128)(2,1)S(1)} %copy-done.1), channel_id=1, replica_groups=mesh['aux'=128,'occ'=4] {'occ'}, dimensions={0}, use_global_device_ids=true | all-gather | bytes 737280 | tf_op jit(solution)/shard_map/all_gather | solution.py:32
  48.9 0.1 broadcast_bitcast_fusion
  49.0 212.3 %all-gather.3.cloned.1.call-done = bf16[128,18,384]{2,1,0:T(8,128)(2,1)} async-done(((bf16[1,18,384]{2,1,0:T(8,128)(2,1)}), bf16[128,18,384]{2,1,0:T(8,128)(2,1)}) %all-gather.3.cloned.1.call-update) | async-done | bytes 1769488 | tf_op jit(solution)/shard_map/all_gather | solution.py:29
  261.3 2.6 reshape.17
  264.0 0.0 copy-done
  264.0 0.3 fusion.3
  264.3 0.1 dot_general.13
  264.5 1.8 fusion
  (2 shorter events, 0.0 us)
Async XLA Ops:
  6.5 257.4 %copy-start = (bf16[18,2304]{1,0:T(8,128)(2,1)S(1)}, bf16[18,2304]{1,0:T(8,128)(2,1)}, u32[]{:S(2)}) copy-start(bf16[18,2304]{1,0:T(8,128)(2,1)} %param.7) | copy-start | bytes 248836
  6.5 33.2 %reduce-scatter.2.cloned.1.call-start = ((), (), s32[]{:S(2)}) async-start(), calls=%async_computation.1 | async-start | bytes 184320 | tf_op jit(solution)/shard_map/reduce_scatter | solution.py:24
  7.5 33.7 %copy-start.1 = (bf16[1536,48]{0,1:T(8,128)(2,1)S(1)}, bf16[1536,48]{0,1:T(8,128)(2,1)}, u32[]{:S(2)}) copy-start(bf16[1536,48]{0,1:T(8,128)(2,1)} %param.5) | copy-start | bytes 442372
  10.6 250.8 %all-gather.3.cloned.1.call-start = ((), (), s32[]{:S(2)}) async-start(), calls=%async_computation.2 | async-start | bytes 2377728 | tf_op jit(solution)/shard_map/all_gather | solution.py:29
Sparse Core Ops, SparseCore 0:
  10.7 29.0 reduce-scatter.1
  44.2 217.0 all-gather.2
where the time goes:
time: 273 us
  waiting for transfers between devices  241 us (88%)
  between operations  13.5 us (5%)
  blocking collectives  7.67 us (3%)
  matrix products  4.27 us (2%)
  local copies, waits for them, and re-layouts  4.02 us (1%)
    all_gather x1, waiting for transfers between devices, on_device(): lax.all_gather(half_transformed, 'aux', axis=0, tiled=True)  212 us
    reduce_scatter x1, waiting for transfers between devices, on_device(): lax.psum_scatter(partial_value, 'occ', scatter_dimension=1, tiled=True)  29.2 us
    all_gather x1, blocking collectives, on_device(): whole_coefficients = lax.all_gather(coefficients, 'occ', axis=0, tiled=True)  7.67 us
  transfers between devices with their start and end apart: 2, of which 2 were waited for; matrix products, arithmetic and copies ran while one was open for 0% of the time, Pallas kernels for 0%

commit v1 on v0

v1 whole, which is shorter than its diff:
```python
import jax
import jax.numpy as jnp
from jax import lax
from jax.experimental import pallas as pl
from jax.experimental.pallas import tpu as pltpu
from jax.sharding import PartitionSpec as P

MESH = pl.DeviceIdType.MESH
BF = jnp.bfloat16
F32 = jnp.float32
TILE = 128

AUX = 18
ROWS = 32
MU = 8
OCC = 48
NU = 1536
NBF = 6144
LANES = 128
CHUNKS = 3
R = 64
PIECE = 16 * AUX
PIECE_PAD = 384
PIECE_ROWS = 32
STEPS = 3
STEP_AUX = AUX // STEPS
STEP_ROWS = STEP_AUX * ROWS


def iota(shape, dim):
    return lax.broadcasted_iota(jnp.int32, shape, dim)


def one_hot(cond):
    return jnp.where(cond, 1.0, 0.0).astype(F32).astype(BF)


def nn(a, b):
    return jnp.dot(a, b, preferred_element_type=F32)


def nt(a, b):
    return lax.dot_general(a, b, (((1,), (1,)), ((), ())), preferred_element_type=F32)


def transform_kernel(
    integrals, coef_t, screening, metric,
    fitted_out, coef_out, screen_out,
    ints, coef, mets, pieces, spread, parts, sends, recv1, half, halves, mrecv, mexp, fsend, recv3, fit,
    load_sem, coef_send, coef_recv, msend, mrecv_sem, send1, recv1_sem, send2, recv2_sem, send3, recv3_sem,
):
    aux = lax.axis_index("aux")
    occ = lax.axis_index("occ")
    z, xh, y = aux // 8, (aux // 4) % 2, aux % 4
    xl, core = occ // 2, occ % 2
    upper = z % 2
    sign = 2 * upper - 1
    place = upper * 8 + xh * 4 + y

    def at_z(distance):
        other = lax.rem(z + distance + 16, 16)
        return {"aux": other * 8 + xh * 4 + y, "occ": occ}

    def mate(k):
        other = lax.rem(xl + k // 2, 2) * 2 + lax.rem(core + k % 2, 2)
        return other

    def near(k):
        zp, xx, yy = lax.rem(upper + k // 8, 2), lax.rem(xh + (k // 4) % 2, 2), lax.rem(y + k % 4, 4)
        return (z - upper + zp) * 8 + xx * 4 + yy, zp * 8 + xx * 4 + yy

    def near_from(k):
        zp, xx, yy = lax.rem(upper + k // 8, 2), lax.rem(xh + (k // 4) % 2, 2), lax.rem(y + 4 - k % 4, 4)
        return (z - upper + zp) * 8 + xx * 4 + yy, zp * 8 + xx * 4 + yy

    barrier = pltpu.get_barrier_semaphore()
    for k in range(1, 4):
        pl.semaphore_signal(barrier, inc=1, device_id={"aux": aux, "occ": mate(k)}, device_id_type=MESH)
    for k in range(1, 16):
        pl.semaphore_signal(barrier, inc=1, device_id={"aux": near_from(k)[0], "occ": occ}, device_id_type=MESH)
    for d in range(1, 8):
        pl.semaphore_signal(barrier, inc=1, device_id=at_z(sign * d), device_id_type=MESH)
    for d in range(2, 8, 2):
        pl.semaphore_signal(barrier, inc=1, device_id=at_z(-sign * d), device_id_type=MESH)

    loads = [pltpu.make_async_copy(coef_t, coef, load_sem.at[STEPS])]
    for j in range(STEPS):
        loads.append(pltpu.make_async_copy(
            integrals.at[pl.ds(j * STEP_AUX, STEP_AUX)], ints.at[pl.ds(j * STEP_AUX, STEP_AUX)], load_sem.at[j]))
    loads.append(pltpu.make_async_copy(metric, mets, load_sem.at[STEPS + 1]))
    for copy in loads:
        copy.start()

    screen = screening[...].astype(F32).astype(BF)
    own_tile = iota((48, NU), 0) == occ * (NU // TILE) + iota((48, NU), 1) // TILE
    mask = nn(screen, one_hot(own_tile)).astype(BF)
    widen = one_hot(iota((OCC, CHUNKS * LANES), 0) == iota((OCC, CHUNKS * LANES), 1) % OCC)
    keep = (iota((ROWS, CHUNKS * LANES), 0) % MU) == (iota((ROWS, CHUNKS * LANES), 1) // OCC)
    keep = jnp.tile(jnp.where(keep, 1.0, 0.0).astype(F32), (STEP_AUX, 1))
    row = iota((4 * R, 1), 0)
    col = iota((1, AUX * ROWS), 1) // MU
    for c in range(CHUNKS):
        p = row % R - AUX * c
        wanted = jnp.where((p >= 0) & (p < AUX), p * 4 + row // R, -1)
        spread[:, c * AUX * ROWS:(c + 1) * AUX * ROWS] = one_hot(wanted == col)
    own_rows = one_hot(iota((16, ROWS), 1) == occ * MU + iota((16, ROWS), 0))
    screen_out[...] = nn(own_rows, screen).astype(BF)

    loads[-1].wait()
    pieces[...] = jnp.zeros_like(pieces)
    for k in range(8):
        pieces[k, 0:AUX, 0:PIECE] = mets[:, k * PIECE:(k + 1) * PIECE]

    loads[0].wait()
    for j in range(STEPS):
        loads[1 + j].wait()
        block = ints[j * STEP_AUX:(j + 1) * STEP_AUX] * mask[None]
        value = nt(block.reshape(STEP_ROWS, NU), coef[...]).astype(BF)
        wide = (nn(value, widen) * keep).astype(BF)
        for c in range(CHUNKS):
            lo = c * AUX * ROWS + j * STEP_ROWS
            parts[lo:lo + STEP_ROWS, :] = wide[:, c * LANES:(c + 1) * LANES]
    sends[...] = nn(spread[...], parts[...]).astype(BF).reshape(4, R, LANES)

    pl.semaphore_wait(barrier, 28)

    first = []
    for k in (3, 2, 1):
        copy = pltpu.make_async_remote_copy(
            src_ref=sends.at[mate(k)], dst_ref=recv1.at[k - 1], send_sem=send1.at[k - 1], recv_sem=recv1_sem.at[k - 1],
            device_id={"aux": aux, "occ": mate(k)}, device_id_type=MESH)
        copy.start()
        first.append(copy)
    metric_copies = []
    for d in (7, 6, 5, 4, 3, 2, 1):
        step = sign * d if d % 2 else -sign * d
        other = lax.rem(z + step + 16, 16)
        copy = pltpu.make_async_remote_copy(
            src_ref=pieces.at[other // 2], dst_ref=mrecv.at[d], send_sem=msend.at[d - 1], recv_sem=mrecv_sem.at[d - 1],
            device_id=at_z(step), device_id_type=MESH)
        copy.start()
        metric_copies.append(copy)
    mrecv[0] = pieces[z // 2]
    for copy in first:
        copy.wait_recv()
    total = sends[occ].astype(F32) + recv1[0].astype(F32) + recv1[1].astype(F32) + recv1[2].astype(F32)
    half[...] = total.astype(BF)

    second = []
    for k in (14, 15, 13, 10, 6, 11, 9, 7, 5, 2, 12, 3, 1, 8, 4):
        copy = pltpu.make_async_remote_copy(
            src_ref=half, dst_ref=halves.at[place], send_sem=send2.at[k - 1], recv_sem=recv2_sem.at[k - 1],
            device_id={"aux": near(k)[0], "occ": occ}, device_id_type=MESH)
        copy.start()
        second.append(copy)
    halves[place] = half[...]

    coef_copies = []
    for k in (3, 2, 1):
        copy = pltpu.make_async_remote_copy(
            src_ref=coef_t, dst_ref=coef_out.at[:, pl.ds(pl.multiple_of(occ * NU, NU), NU)],
            send_sem=coef_send.at[k - 1], recv_sem=coef_recv.at[k - 1],
            device_id={"aux": aux, "occ": mate(k)}, device_id_type=MESH)
        copy.start()
        coef_copies.append(copy)
    own_coef = pltpu.make_async_copy(coef, coef_out.at[:, pl.ds(pl.multiple_of(occ * NU, NU), NU)], load_sem.at[0])
    own_coef.start()

    for copy in metric_copies:
        copy.wait_recv()
    c_of_col = iota((PIECE_PAD, 16 * R), 1) % R
    source = (iota((PIECE_PAD, 16 * R), 1) // R) * AUX + c_of_col % AUX
    columns = one_hot((iota((PIECE_PAD, 16 * R), 0) == source) & (c_of_col < CHUNKS * AUX))
    wide_metric = nn(mrecv[...].reshape(8 * PIECE_ROWS, PIECE_PAD), columns).astype(BF)
    r_of_row = iota((8 * R, 1), 0) % R
    source = jnp.where(r_of_row < CHUNKS * AUX, (iota((8 * R, 1), 0) // R) * PIECE_ROWS + r_of_row % AUX, -1)
    rows = one_hot(source == iota((1, 8 * PIECE_ROWS), 1))
    same = (r_of_row // AUX) == ((iota((1, 16 * R), 1) % R) // AUX)
    mexp[...] = jnp.where(same, nn(rows, wide_metric), 0.0).astype(BF)

    for copy in second:
        copy.wait_recv()
    partial = nn(mexp[...], halves[...].reshape(16 * R, LANES)).reshape(8, R, LANES)
    fit[...] = partial[0]
    fsend[...] = partial.astype(BF)

    third = []
    for d in (7, 6, 5, 4, 3, 2, 1):
        copy = pltpu.make_async_remote_copy(
            src_ref=fsend.at[d], dst_ref=recv3.at[d - 1], send_sem=send3.at[d - 1], recv_sem=recv3_sem.at[d - 1],
            device_id=at_z(sign * d), device_id_type=MESH)
        copy.start()
        third.append(copy)
    for copy in third[::-1]:
        copy.wait_recv()
    total = fit[...]
    for d in range(7):
        total = total + recv3[d].astype(F32)
    fitted = total.astype(BF)

    wide_rows = iota((AUX * MU, R), 0)
    out = None
    for c in range(CHUNKS):
        pick = one_hot(iota((AUX * MU, R), 1) == wide_rows // MU + c * AUX)
        value = nn(pick, fitted)
        lane = iota((AUX * MU, LANES), 1) + c * LANES
        value = jnp.where(lane // OCC == iota((AUX * MU, LANES), 0) % MU, value, 0.0).astype(BF)
        fold = one_hot((iota((LANES, LANES), 0) + c * LANES) % OCC == iota((LANES, LANES), 1))
        value = nn(value, fold)
        out = value if out is None else out + value
    fitted_out[...] = out.astype(BF)

    own_coef.wait()
    for copy in coef_copies:
        copy.wait_recv()
    for copy in first + metric_copies + second + coef_copies + third:
        copy.wait_send()


def gamma_kernel(fitted, coef, screen, out):
    width = out.shape[2]
    tile = pl.program_id(0) * (width // TILE) + iota((48, width), 1) // TILE
    mask = nn(screen[...], one_hot(iota((48, width), 0) == tile))[0:MU]
    product = nn(fitted[...][:, 0:OCC], coef[...])
    out[...] = (product.reshape(AUX, MU, width) * mask[None]).astype(BF)


def on_device(integrals, coefficients, screening, metric_factor):
    hbm = pl.BlockSpec(memory_space=pl.ANY)
    vmem = pl.BlockSpec(memory_space=pltpu.VMEM)
    dma = pltpu.SemaphoreType.DMA
    fitted, coef_all, own_screen = pl.pallas_call(
        transform_kernel,
        name="exchange",
        out_shape=(
            jax.ShapeDtypeStruct((AUX * MU, LANES), BF),
            jax.ShapeDtypeStruct((OCC, NBF), BF),
            jax.ShapeDtypeStruct((16, 48), BF),
        ),
        in_specs=[hbm, hbm, vmem, hbm],
        out_specs=(vmem, hbm, vmem),
        scratch_shapes=[
            pltpu.VMEM((AUX, ROWS, NU), BF),
            pltpu.VMEM((OCC, NU), BF),
            pltpu.VMEM((AUX, 2304), BF),
            pltpu.VMEM((8, PIECE_ROWS, PIECE_PAD), BF),
            pltpu.VMEM((4 * R, CHUNKS * AUX * ROWS), BF),
            pltpu.VMEM((CHUNKS * AUX * ROWS, LANES), BF),
            pltpu.VMEM((4, R, LANES), BF),
            pltpu.VMEM((3, R, LANES), BF),
            pltpu.VMEM((R, LANES), BF),
            pltpu.VMEM((16, R, LANES), BF),
            pltpu.VMEM((8, PIECE_ROWS, PIECE_PAD), BF),
            pltpu.VMEM((8 * R, 16 * R), BF),
            pltpu.VMEM((8, R, LANES), BF),
            pltpu.VMEM((7, R, LANES), BF),
            pltpu.VMEM((R, LANES), F32),
            dma((STEPS + 2,)),
            dma((3,)), dma((3,)),
            dma((7,)), dma((7,)),
            dma((3,)), dma((3,)),
            dma((15,)), dma((15,)),
            dma((7,)), dma((7,)),
        ],
        compiler_params=pltpu.CompilerParams(collective_id=0, has_side_effects=True),
    )(integrals, coefficients.T, screening, metric_factor)
    width = 1024
    return pl.pallas_call(
        gamma_kernel,
        name="gamma",
        grid=(NBF // width,),
        out_shape=jax.ShapeDtypeStruct((AUX, MU, NBF), BF),
        in_specs=[
            pl.BlockSpec((AUX * MU, LANES), lambda j: (0, 0)),
            pl.BlockSpec((OCC, width), lambda j: (0, j)),
            pl.BlockSpec((16, 48), lambda j: (0, 0)),
        ],
        out_specs=pl.BlockSpec((AUX, MU, width), lambda j: (0, 0, j)),
    )(fitted, coef_all, own_screen)


def solution(mesh):
    return jax.shard_map(
        on_device,
        mesh=mesh,
        in_specs=(P("aux", None, "occ"), P("occ", None), P(), P("aux", None)),
        out_specs=P("aux", "occ", None),
        check_vma=False,
    )
```

time: 273 us -> 43.2 us (0.16)
  the two profiles are of different devices: /device:TPU:8 before, /device:TPU:1 now
where the time goes in v1:
time: 43.2 us; the launch traced here: 42.8 us
  Pallas kernels  42.8 us (99%)
    pallas_call x1, Pallas kernels, on_device(): pl.pallas_call(transform_kernel, name='exchange', out_shape=(jax.ShapeDty...  37.8 us
    pallas_call x1, Pallas kernels, on_device(): pl.pallas_call(gamma_kernel, name='gamma', grid=(NBF // width,), out_shap...  4.96 us

profile of v1, /device:TPU:1, one launch (start us, length us, event | category | flops | bytes accessed | tf_op | source)
XLA Modules:
  0.0 42.8 jit_solution(18209623209381977923)
XLA Ops:
  0.0 37.8 %exchange.1 = (bf16[144,128]{1,0:T(8,128)(2,1)}, bf16[48,6144]{1,0:T(8,128)(2,1)}, bf16[16,48]{1,0:T(8,128)(2,1)}) custom-call(bf16[18,32,1536]{2,1,0:T(8,128)(2,1)} %integrals.1, bf16[48,1536]{1,0:T(8,128)(2,1)} %bitcast.1, s32[32,48]{1,0:T(8,128)} %screening.1, bf16[18,2304]{1,0:T(8,128)(2,1)} %metric.1), custom_call_target="tpu_custom_call" | custom-call | tf_op jit(solution)/shard_map/exchange/pallas_call | solution.py:232
  37.8 5.0 %gamma.1 = bf16[18,8,6144]{2,1,0:T(8,128)(2,1)} custom-call(bf16[144,128]{1,0:T(8,128)(2,1)} %get-tuple-element.8.fitted, bf16[48,6144]{1,0:T(8,128)(2,1)} %get-tuple-element.9.coef, bf16[16,48]{1,0:T(8,128)(2,1)} %get-tuple-element.10.screen), custom_call_target="tpu_custom_call" | custom-call | tf_op jit(solution)/shard_map/gamma/pallas_call | solution.py:268

commit v2 on v1

v2 whole, which is shorter than its diff:
```python
import jax
import jax.numpy as jnp
from jax import lax
from jax.experimental import pallas as pl
from jax.experimental.pallas import tpu as pltpu
from jax.sharding import PartitionSpec as P

MESH = pl.DeviceIdType.MESH
BF = jnp.bfloat16
F32 = jnp.float32
TILE = 128

AUX = 18
ROWS = 32
MU = 8
OCC = 48
NU = 1536
NBF = 6144
LANES = 128
CHUNKS = 3
R = 56
PIECE = 16 * AUX
PIECE_PAD = 384
PIECE_ROWS = 24
STEPS = 3
STEP_AUX = AUX // STEPS
STEP_ROWS = STEP_AUX * ROWS
GAMMA_STEPS = 6
EARLY = (7, 6, 5, 4, 3, 2, 1)
LATE = ()


def iota(shape, dim):
    return lax.broadcasted_iota(jnp.int32, shape, dim)


def one_hot(cond):
    return jnp.where(cond, 1.0, 0.0).astype(F32).astype(BF)


def nn(a, b):
    return jnp.dot(a, b, preferred_element_type=F32)


def nt(a, b):
    return lax.dot_general(a, b, (((1,), (1,)), ((), ())), preferred_element_type=F32)


def exchange_kernel(
    integrals, coef_t, screening, metric,
    fitted_out, coef_out, mask_out,
    ints, coef, mets, scr, pieces, spread, parts, sends, recv1, half, halves, mrecv, columns, rows, mexp, fsend, recv3, fit, pick, lanes, fold,
    load_sem, coef_send, coef_recv, msend, mrecv_sem, send1, recv1_sem, send2, recv2_sem, send3, recv3_sem,
):
    aux = lax.axis_index("aux")
    occ = lax.axis_index("occ")
    z, xh, y = aux // 8, (aux // 4) % 2, aux % 4
    xl, core = occ // 2, occ % 2
    upper = z % 2
    sign = 2 * upper - 1
    place = upper * 8 + xh * 4 + y

    def at_z(distance):
        other = lax.rem(z + distance + 16, 16)
        return {"aux": other * 8 + xh * 4 + y, "occ": occ}

    def mate(k):
        return lax.rem(xl + k // 2, 2) * 2 + lax.rem(core + k % 2, 2)

    def near(k, way):
        zp, xx, yy = lax.rem(upper + k // 8, 2), lax.rem(xh + (k // 4) % 2, 2), lax.rem(y + 4 + way * (k % 4), 4)
        return {"aux": (z - upper + zp) * 8 + xx * 4 + yy, "occ": occ}

    loads = [pltpu.make_async_copy(screening, scr, load_sem.at[0]), pltpu.make_async_copy(coef_t, coef, load_sem.at[1])]
    for j in range(STEPS):
        part = pl.ds(j * STEP_AUX, STEP_AUX)
        loads.append(pltpu.make_async_copy(integrals.at[part], ints.at[part], load_sem.at[2 + j]))
    loads.append(pltpu.make_async_copy(metric, mets, load_sem.at[2 + STEPS]))
    for copy in loads:
        copy.start()

    barrier = pltpu.get_barrier_semaphore()
    for k in range(1, 4):
        pl.semaphore_signal(barrier, inc=1, device_id={"aux": aux, "occ": mate(k)}, device_id_type=MESH)
    for k in range(1, 16):
        pl.semaphore_signal(barrier, inc=1, device_id=near(k, -1), device_id_type=MESH)
    for d in range(1, 8):
        pl.semaphore_signal(barrier, inc=1, device_id=at_z(sign * d), device_id_type=MESH)
    for d in range(2, 8, 2):
        pl.semaphore_signal(barrier, inc=1, device_id=at_z(-sign * d), device_id_type=MESH)

    widen = one_hot(iota((OCC, CHUNKS * LANES), 0) == iota((OCC, CHUNKS * LANES), 1) % OCC)
    keep = (iota((ROWS, CHUNKS * LANES), 0) % MU) == (iota((ROWS, CHUNKS * LANES), 1) // OCC)
    keep = jnp.tile(jnp.where(keep, 1.0, 0.0).astype(F32), (STEP_AUX, 1))
    row = iota((4 * R, 1), 0)
    col = iota((1, AUX * ROWS), 1) // MU
    for c in range(CHUNKS):
        p = row % R - AUX * c
        wanted = jnp.where((p >= 0) & (p < AUX), p * 4 + row // R, -1)
        spread[:, c * AUX * ROWS:(c + 1) * AUX * ROWS] = one_hot(wanted == col)
    own_tile = one_hot(iota((48, NU), 0) == occ * (NU // TILE) + iota((48, NU), 1) // TILE)
    loads[0].wait()
    screen = scr[...].astype(F32).astype(BF)
    mask = nn(screen, own_tile).astype(BF)

    loads[1].wait()
    for j in range(STEPS):
        loads[2 + j].wait()
        block = ints[j * STEP_AUX:(j + 1) * STEP_AUX] * mask[None]
        value = nt(block.reshape(STEP_ROWS, NU), coef[...]).astype(BF)
        wide = (nn(value, widen) * keep).astype(BF)
        for c in range(CHUNKS):
            lo = c * AUX * ROWS + j * STEP_ROWS
            parts[lo:lo + STEP_ROWS, :] = wide[:, c * LANES:(c + 1) * LANES]
    sends[...] = nn(spread[...], parts[...]).astype(BF).reshape(4, R, LANES)

    pl.semaphore_wait(barrier, 28)

    first = []
    for k in (3, 2, 1):
        copy = pltpu.make_async_remote_copy(
            src_ref=sends.at[mate(k)], dst_ref=recv1.at[k - 1], send_sem=send1.at[k - 1], recv_sem=recv1_sem.at[k - 1],
            device_id={"aux": aux, "occ": mate(k)}, device_id_type=MESH)
        copy.start()
        first.append(copy)

    loads[-1].wait()
    pieces[...] = jnp.zeros_like(pieces)
    for k in range(8):
        pieces[k, 0:AUX, 0:PIECE] = mets[:, k * PIECE:(k + 1) * PIECE]

    def send_metric(d):
        step = sign * d if d % 2 else -sign * d
        other = lax.rem(z + step + 16, 16)
        copy = pltpu.make_async_remote_copy(
            src_ref=pieces.at[other // 2], dst_ref=mrecv.at[d], send_sem=msend.at[d - 1], recv_sem=mrecv_sem.at[d - 1],
            device_id=at_z(step), device_id_type=MESH)
        copy.start()
        return copy

    metric_copies = [send_metric(d) for d in EARLY]
    mrecv[0] = pieces[z // 2]
    for copy in first:
        copy.wait_recv()
    total = sends[occ].astype(F32) + recv1[0].astype(F32) + recv1[1].astype(F32) + recv1[2].astype(F32)
    half[...] = total.astype(BF)

    second = []
    for k in (14, 13, 15, 6, 10, 12, 5, 7, 9, 11, 2, 4, 1, 3, 8):
        copy = pltpu.make_async_remote_copy(
            src_ref=half, dst_ref=halves.at[place], send_sem=send2.at[k - 1], recv_sem=recv2_sem.at[k - 1],
            device_id=near(k, 1), device_id_type=MESH)
        copy.start()
        second.append(copy)
    metric_copies += [send_metric(d) for d in LATE]
    halves[place] = half[...]

    own_nu = pl.ds(pl.multiple_of(occ * NU, NU), NU)
    to_core = pltpu.make_async_remote_copy(
        src_ref=coef_t, dst_ref=coef_out.at[:, own_nu], send_sem=coef_send.at[0], recv_sem=coef_recv.at[0],
        device_id={"aux": aux, "occ": mate(1)}, device_id_type=MESH)
    to_core.start()
    to_chip = pltpu.make_async_remote_copy(
        src_ref=coef_t, dst_ref=coef_out.at[:, own_nu], send_sem=coef_send.at[1], recv_sem=coef_recv.at[1],
        device_id={"aux": aux, "occ": mate(2)}, device_id_type=MESH)
    to_chip.start()
    own_coef = pltpu.make_async_copy(coef, coef_out.at[:, own_nu], load_sem.at[0])
    own_coef.start()

    c_of_col = iota((PIECE_PAD, 16 * R), 1) % R
    source = (iota((PIECE_PAD, 16 * R), 1) // R) * AUX + c_of_col % AUX
    columns[...] = one_hot((iota((PIECE_PAD, 16 * R), 0) == source) & (c_of_col < CHUNKS * AUX))
    r_of_row = iota((8 * R, 1), 0) % R
    source = jnp.where(r_of_row < CHUNKS * AUX, (iota((8 * R, 1), 0) // R) * PIECE_ROWS + r_of_row % AUX, -1)
    rows[...] = one_hot(source == iota((1, 8 * PIECE_ROWS), 1))
    row = iota((AUX * MU, 1), 0)
    for c in range(CHUNKS):
        pick[c * AUX * MU:(c + 1) * AUX * MU, :] = one_hot(iota((1, R), 1) == row // MU + c * AUX)
        lanes[c * AUX * MU:(c + 1) * AUX * MU, :] = jnp.where(
            (iota((1, LANES), 1) + c * LANES) // OCC == row % MU, 1.0, 0.0).astype(F32)
    fold[...] = one_hot(iota((CHUNKS * LANES, OCC), 0) % OCC == iota((CHUNKS * LANES, OCC), 1))
    own_rows = one_hot(iota((16, ROWS), 1) == occ * MU + iota((16, ROWS), 0) % MU)
    own_screen = nn(own_rows, screen).astype(BF)
    for k in range(4):
        tile = one_hot(iota((48, NU), 0) == k * (NU // TILE) + iota((48, NU), 1) // TILE)
        mask_out[:, k * NU:(k + 1) * NU] = nn(own_screen, tile)[0:MU]

    for copy in metric_copies:
        copy.wait_recv()
    wide_metric = nn(mrecv[...].reshape(8 * PIECE_ROWS, PIECE_PAD), columns[...]).astype(BF)
    same = ((iota((8 * R, 1), 0) % R) // AUX) == ((iota((1, 16 * R), 1) % R) // AUX)
    mexp[...] = jnp.where(same, nn(rows[...], wide_metric), 0.0).astype(BF)

    for copy in second:
        copy.wait_recv()
    partial = nn(mexp[...], halves[...].reshape(16 * R, LANES)).reshape(8, R, LANES)
    fsend[...] = partial.astype(BF)

    third = []
    for d in (7, 6, 5, 4, 3, 2, 1):
        copy = pltpu.make_async_remote_copy(
            src_ref=fsend.at[d], dst_ref=recv3.at[d - 1], send_sem=send3.at[d - 1], recv_sem=recv3_sem.at[d - 1],
            device_id=at_z(sign * d), device_id_type=MESH)
        copy.start()
        third.append(copy)
    fit[...] = partial[0]

    to_chip.wait_recv()
    chip_nu = pl.ds(pl.multiple_of(mate(2) * NU, NU), NU)
    onward = pltpu.make_async_remote_copy(
        src_ref=coef_out.at[:, chip_nu], dst_ref=coef_out.at[:, chip_nu], send_sem=coef_send.at[2], recv_sem=coef_recv.at[2],
        device_id={"aux": aux, "occ": mate(1)}, device_id_type=MESH)
    onward.start()

    total = fit[...]
    for d in range(1, 8):
        third[7 - d].wait_recv()
        total = total + recv3[d - 1].astype(F32)

    value = (nn(pick[...], total.astype(BF)) * lanes[...]).astype(BF)
    value = jnp.concatenate([value[c * AUX * MU:(c + 1) * AUX * MU] for c in range(CHUNKS)], axis=1)
    fitted_out[...] = nn(value, fold[...]).astype(BF)

    own_coef.wait()
    to_core.wait_recv()
    onward.wait_recv()
    for copy in first + metric_copies + second + third + [to_core, to_chip, onward]:
        copy.wait_send()


def gamma_kernel(fitted, coef, mask, out, buffer, sems):
    width = NBF // sems.shape[0]
    copies = []
    for k in range(sems.shape[0]):
        part = pl.ds(k * width, width)
        product = nn(fitted[...], coef[:, k * width:(k + 1) * width])
        scaled = product.reshape(AUX, MU, width) * mask[:, k * width:(k + 1) * width][None]
        buffer[:, k * width:(k + 1) * width] = scaled.reshape(AUX * MU, width).astype(BF)
        copies.append(pltpu.make_async_copy(buffer.at[:, part], out.at[:, part], sems.at[k]))
        copies[-1].start()
    for copy in copies:
        copy.wait()


def on_device(integrals, coefficients, screening, metric_factor):
    hbm = pl.BlockSpec(memory_space=pltpu.HBM)
    free = pl.BlockSpec(memory_space=pl.ANY)
    vmem = pl.BlockSpec(memory_space=pltpu.VMEM)
    dma = pltpu.SemaphoreType.DMA
    fitted, coef_all, mask = pl.pallas_call(
        exchange_kernel,
        name="exchange",
        out_shape=(
            jax.ShapeDtypeStruct((AUX * MU, OCC), BF),
            jax.ShapeDtypeStruct((OCC, NBF), BF),
            jax.ShapeDtypeStruct((MU, NBF), F32),
        ),
        in_specs=[hbm, hbm, hbm, hbm],
        out_specs=(vmem, free, vmem),
        scratch_shapes=[
            pltpu.VMEM((AUX, ROWS, NU), BF),
            pltpu.VMEM((OCC, NU), BF),
            pltpu.VMEM((AUX, 2304), BF),
            pltpu.VMEM((ROWS, 48), jnp.int32),
            pltpu.VMEM((8, PIECE_ROWS, PIECE_PAD), BF),
            pltpu.VMEM((4 * R, CHUNKS * AUX * ROWS), BF),
            pltpu.VMEM((CHUNKS * AUX * ROWS, LANES), BF),
            pltpu.VMEM((4, R, LANES), BF),
            pltpu.VMEM((3, R, LANES), BF),
            pltpu.VMEM((R, LANES), BF),
            pltpu.VMEM((16, R, LANES), BF),
            pltpu.VMEM((8, PIECE_ROWS, PIECE_PAD), BF),
            pltpu.VMEM((PIECE_PAD, 16 * R), BF),
            pltpu.VMEM((8 * R, 8 * PIECE_ROWS), BF),
            pltpu.VMEM((8 * R, 16 * R), BF),
            pltpu.VMEM((8, R, LANES), BF),
            pltpu.VMEM((7, R, LANES), BF),
            pltpu.VMEM((R, LANES), F32),
            pltpu.VMEM((CHUNKS * AUX * MU, R), BF),
            pltpu.VMEM((CHUNKS * AUX * MU, LANES), F32),
            pltpu.VMEM((CHUNKS * LANES, OCC), BF),
            dma((STEPS + 3,)),
            dma((3,)), dma((3,)),
            dma((7,)), dma((7,)),
            dma((3,)), dma((3,)),
            dma((15,)), dma((15,)),
            dma((7,)), dma((7,)),
        ],
        compiler_params=pltpu.CompilerParams(collective_id=0, has_side_effects=True, vmem_limit_bytes=24 * 1024 * 1024),
    )(*(pltpu.with_memory_space_constraint(a, pltpu.HBM) for a in (integrals, coefficients.T, screening, metric_factor)))
    gamma = pl.pallas_call(
        gamma_kernel,
        name="gamma",
        out_shape=jax.ShapeDtypeStruct((AUX * MU, NBF), BF),
        in_specs=[vmem, vmem, vmem],
        out_specs=hbm,
        scratch_shapes=[pltpu.VMEM((AUX * MU, NBF), BF), dma((GAMMA_STEPS,))],
        compiler_params=pltpu.CompilerParams(vmem_limit_bytes=16 * 1024 * 1024),
    )(fitted, coef_all, mask)
    return gamma.reshape(AUX, MU, NBF)


def solution(mesh):
    return jax.shard_map(
        on_device,
        mesh=mesh,
        in_specs=(P("aux", None, "occ"), P("occ", None), P(), P("aux", None)),
        out_specs=P("aux", "occ", None),
        check_vma=False,
    )
```

time: 43.2 us -> 35.8 us (0.83)
  the two profiles are of different devices: /device:TPU:1 before, /device:TPU:2 now
where the time goes in v2:
time: 35.8 us; the launch traced here: 35.6 us
  Pallas kernels  35.6 us (99%)
    pallas_call x1, Pallas kernels, on_device(): pl.pallas_call(exchange_kernel, name='exchange', out_shape=(jax.ShapeDtyp...  34.1 us
    pallas_call x1, Pallas kernels, on_device(): pl.pallas_call(gamma_kernel, name='gamma', out_shape=jax.ShapeDtypeStruct...  1.48 us

profile of v2, /device:TPU:2, one launch (start us, length us, event | category | flops | bytes accessed | tf_op | source)
XLA Modules:
  0.0 35.6 jit_solution(1089690852808987913)
XLA Ops:
  0.0 34.1 %exchange.1 = (bf16[144,48]{1,0:T(8,128)(2,1)S(1)}, bf16[48,6144]{1,0:T(8,128)(2,1)S(1)}, f32[8,6144]{1,0:T(8,128)S(1)}) custom-call(bf16[18,32,1536]{2,1,0:T(8,128)(2,1)} %integrals.1, bf16[48,1536]{1,0:T(8,128)(2,1)} %bitcast.2, s32[32,48]{1,0:T(8,128)} %screening.1, bf16[18,2304]{1,0:T(8,128)(2,1)} %metric.1), custom_call_target="tpu_custom_call" | custom-call | tf_op jit(solution)/shard_map/exchange/pallas_call | solution.py:250
  34.1 1.5 %gamma.1 = bf16[144,6144]{1,0:T(8,128)(2,1)} custom-call(bf16[144,48]{1,0:T(8,128)(2,1)S(1)} %get-tuple-element.8.fitted, bf16[48,6144]{1,0:T(8,128)(2,1)S(1)} %get-tuple-element.9.coef, f32[8,6144]{1,0:T(8,128)S(1)} %get-tuple-element.10.mask), custom_call_target="tpu_custom_call" | custom-call | tf_op jit(solution)/shard_map/gamma/pallas_call | solution.py:291

commit v3 on v2

--- a/solution.py
+++ b/solution.py
@@ -26,8 +26,7 @@
 STEP_AUX = AUX // STEPS
 STEP_ROWS = STEP_AUX * ROWS
 GAMMA_STEPS = 6
-EARLY = (7, 6, 5, 4, 3, 2, 1)
-LATE = ()
+METRIC_ORDER = ((6, 4, 2), (7, 5, 3, 1))
 
 
 def iota(shape, dim):
@@ -49,8 +48,8 @@
 def exchange_kernel(
     integrals, coef_t, screening, metric,
     fitted_out, coef_out, mask_out,
-    ints, coef, mets, scr, pieces, spread, parts, sends, recv1, half, halves, mrecv, columns, rows, mexp, fsend, recv3, fit, pick, lanes, fold,
-    load_sem, coef_send, coef_recv, msend, mrecv_sem, send1, recv1_sem, send2, recv2_sem, send3, recv3_sem,
+    ints, coef, coef_n, values, mets, scr, pieces, spread, parts, sends, recv1, half, halves, mrecv, columns, rows, mexp, fsend, recv3, fit, pick, lanes, fold,
+    load_sem, coef_send, coef_recv, msend, mrecv_sem, fsend_sem, send1, recv1_sem, send2, recv2_sem, send3, recv3_sem,
 ):
     aux = lax.axis_index("aux")
     occ = lax.axis_index("occ")
@@ -71,12 +70,15 @@
         zp, xx, yy = lax.rem(upper + k // 8, 2), lax.rem(xh + (k // 4) % 2, 2), lax.rem(y + 4 + way * (k % 4), 4)
         return {"aux": (z - upper + zp) * 8 + xx * 4 + yy, "occ": occ}
 
-    loads = [pltpu.make_async_copy(screening, scr, load_sem.at[0]), pltpu.make_async_copy(coef_t, coef, load_sem.at[1])]
+    loads = [
+        pltpu.make_async_copy(screening, scr, load_sem.at[0]),
+        pltpu.make_async_copy(coef_t, coef, load_sem.at[1]),
+    ]
     for j in range(STEPS):
         part = pl.ds(j * STEP_AUX, STEP_AUX)
         loads.append(pltpu.make_async_copy(integrals.at[part], ints.at[part], load_sem.at[2 + j]))
     loads.append(pltpu.make_async_copy(metric, mets, load_sem.at[2 + STEPS]))
-    for copy in loads:
+    for copy in loads[:2] + loads[-1:] + loads[2:-1]:
         copy.start()
 
     barrier = pltpu.get_barrier_semaphore()
@@ -91,7 +93,7 @@
 
     widen = one_hot(iota((OCC, CHUNKS * LANES), 0) == iota((OCC, CHUNKS * LANES), 1) % OCC)
     keep = (iota((ROWS, CHUNKS * LANES), 0) % MU) == (iota((ROWS, CHUNKS * LANES), 1) // OCC)
-    keep = jnp.tile(jnp.where(keep, 1.0, 0.0).astype(F32), (STEP_AUX, 1))
+    keep = jnp.tile(jnp.where(keep, 1.0, 0.0).astype(F32), (AUX, 1))
     row = iota((4 * R, 1), 0)
     col = iota((1, AUX * ROWS), 1) // MU
     for c in range(CHUNKS):
@@ -103,15 +105,21 @@
     screen = scr[...].astype(F32).astype(BF)
     mask = nn(screen, own_tile).astype(BF)
 
+    loads[-1].wait()
+    pieces[...] = jnp.zeros_like(pieces)
+    for k in range(8):
+        pieces[k, 0:AUX, 0:PIECE] = mets[:, k * PIECE:(k + 1) * PIECE]
+    mrecv[0] = pieces[z // 2]
+
     loads[1].wait()
+    coef_n[...] = coef[...].T
     for j in range(STEPS):
         loads[2 + j].wait()
         block = ints[j * STEP_AUX:(j + 1) * STEP_AUX] * mask[None]
-        value = nt(block.reshape(STEP_ROWS, NU), coef[...]).astype(BF)
-        wide = (nn(value, widen) * keep).astype(BF)
-        for c in range(CHUNKS):
-            lo = c * AUX * ROWS + j * STEP_ROWS
-            parts[lo:lo + STEP_ROWS, :] = wide[:, c * LANES:(c + 1) * LANES]
+        values[j * STEP_ROWS:(j + 1) * STEP_ROWS, :] = nn(block.reshape(STEP_ROWS, NU), coef_n[...]).astype(BF)
+    wide = (nn(values[...], widen) * keep).astype(BF)
+    for c in range(CHUNKS):
+        parts[c * AUX * ROWS:(c + 1) * AUX * ROWS, :] = wide[:, c * LANES:(c + 1) * LANES]
     sends[...] = nn(spread[...], parts[...]).astype(BF).reshape(4, R, LANES)
 
     pl.semaphore_wait(barrier, 28)
@@ -124,22 +132,23 @@
         copy.start()
         first.append(copy)
 
-    loads[-1].wait()
-    pieces[...] = jnp.zeros_like(pieces)
-    for k in range(8):
-        pieces[k, 0:AUX, 0:PIECE] = mets[:, k * PIECE:(k + 1) * PIECE]
-
-    def send_metric(d):
+    def metric_copy(d):
         step = sign * d if d % 2 else -sign * d
         other = lax.rem(z + step + 16, 16)
-        copy = pltpu.make_async_remote_copy(
+        return pltpu.make_async_remote_copy(
             src_ref=pieces.at[other // 2], dst_ref=mrecv.at[d], send_sem=msend.at[d - 1], recv_sem=mrecv_sem.at[d - 1],
             device_id=at_z(step), device_id_type=MESH)
-        copy.start()
-        return copy
-
-    metric_copies = [send_metric(d) for d in EARLY]
-    mrecv[0] = pieces[z // 2]
+
+    def onward_copy(d):
+        return pltpu.make_async_remote_copy(
+            src_ref=mrecv.at[d], dst_ref=mrecv.at[d], send_sem=fsend_sem.at[d - 1], recv_sem=mrecv_sem.at[d - 1],
+            device_id={"aux": aux, "occ": mate(1)}, device_id_type=MESH)
+
+    for turn in range(2):
+        @pl.when(core == turn)
+        def _():
+            for d in METRIC_ORDER[turn]:
+                metric_copy(d).start()
     for copy in first:
         copy.wait_recv()
     total = sends[occ].astype(F32) + recv1[0].astype(F32) + recv1[1].astype(F32) + recv1[2].astype(F32)
@@ -152,7 +161,6 @@
             device_id=near(k, 1), device_id_type=MESH)
         copy.start()
         second.append(copy)
-    metric_copies += [send_metric(d) for d in LATE]
     halves[place] = half[...]
 
     own_nu = pl.ds(pl.multiple_of(occ * NU, NU), NU)
@@ -185,8 +193,14 @@
         tile = one_hot(iota((48, NU), 0) == k * (NU // TILE) + iota((48, NU), 1) // TILE)
         mask_out[:, k * NU:(k + 1) * NU] = nn(own_screen, tile)[0:MU]
 
-    for copy in metric_copies:
-        copy.wait_recv()
+    for turn in range(2):
+        @pl.when(core == turn)
+        def _():
+            for d in METRIC_ORDER[turn][::-1]:
+                metric_copy(d).wait_recv()
+                onward_copy(d).start()
+            for d in METRIC_ORDER[1 - turn][::-1]:
+                metric_copy(d).wait_recv()
     wide_metric = nn(mrecv[...].reshape(8 * PIECE_ROWS, PIECE_PAD), columns[...]).astype(BF)
     same = ((iota((8 * R, 1), 0) % R) // AUX) == ((iota((1, 16 * R), 1) % R) // AUX)
     mexp[...] = jnp.where(same, nn(rows[...], wide_metric), 0.0).astype(BF)
@@ -224,7 +238,13 @@
     own_coef.wait()
     to_core.wait_recv()
     onward.wait_recv()
-    for copy in first + metric_copies + second + third + [to_core, to_chip, onward]:
+    for turn in range(2):
+        @pl.when(core == turn)
+        def _():
+            for d in METRIC_ORDER[turn]:
+                metric_copy(d).wait_send()
+                onward_copy(d).wait_send()
+    for copy in first + second + third + [to_core, to_chip, onward]:
         copy.wait_send()
 
 
@@ -260,6 +280,8 @@
         scratch_shapes=[
             pltpu.VMEM((AUX, ROWS, NU), BF),
             pltpu.VMEM((OCC, NU), BF),
+            pltpu.VMEM((NU, OCC), BF),
+            pltpu.VMEM((AUX * ROWS, OCC), BF),
             pltpu.VMEM((AUX, 2304), BF),
             pltpu.VMEM((ROWS, 48), jnp.int32),
             pltpu.VMEM((8, PIECE_ROWS, PIECE_PAD), BF),
@@ -281,7 +303,7 @@
             pltpu.VMEM((CHUNKS * LANES, OCC), BF),
             dma((STEPS + 3,)),
             dma((3,)), dma((3,)),
-            dma((7,)), dma((7,)),
+            dma((7,)), dma((7,)), dma((7,)),
             dma((3,)), dma((3,)),
             dma((15,)), dma((15,)),
             dma((7,)), dma((7,)),

time: 35.8 us -> 34.5 us (0.964)
  the two profiles are of different devices: /device:TPU:2 before, /device:TPU:8 now
where the time goes in v3:
time: 34.5 us; the launch traced here: 34.3 us
  Pallas kernels  34.3 us (99%)
    pallas_call x1, Pallas kernels, on_device(): pl.pallas_call(exchange_kernel, name='exchange', out_shape=(jax.ShapeDtyp...  32.8 us
    pallas_call x1, Pallas kernels, on_device(): pl.pallas_call(gamma_kernel, name='gamma', out_shape=jax.ShapeDtypeStruct...  1.47 us

profile of v3, /device:TPU:8, one launch (start us, length us, event | category | flops | bytes accessed | tf_op | source)
XLA Modules:
  0.0 34.3 jit_solution(14447951588847117902)
XLA Ops:
  0.0 32.8 %exchange.1 = (bf16[144,48]{1,0:T(8,128)(2,1)S(1)}, bf16[48,6144]{1,0:T(8,128)(2,1)S(1)}, f32[8,6144]{1,0:T(8,128)S(1)}) custom-call(bf16[18,32,1536]{2,1,0:T(8,128)(2,1)} %integrals.1, bf16[48,1536]{1,0:T(8,128)(2,1)} %bitcast.2, s32[32,48]{1,0:T(8,128)} %screening.1, bf16[18,2304]{1,0:T(8,128)(2,1)} %metric.1), custom_call_target="tpu_custom_call" | custom-call | tf_op jit(solution)/shard_map/exchange/pallas_call | solution.py:270
  32.8 1.5 %gamma.1 = bf16[144,6144]{1,0:T(8,128)(2,1)} custom-call(bf16[144,48]{1,0:T(8,128)(2,1)S(1)} %get-tuple-element.8.fitted, bf16[48,6144]{1,0:T(8,128)(2,1)S(1)} %get-tuple-element.9.coef, f32[8,6144]{1,0:T(8,128)S(1)} %get-tuple-element.10.mask), custom_call_target="tpu_custom_call" | custom-call | tf_op jit(solution)/shard_map/gamma/pallas_call | solution.py:313

commit v4 on v3

--- a/solution.py
+++ b/solution.py
@@ -22,9 +22,7 @@
 PIECE = 16 * AUX
 PIECE_PAD = 384
 PIECE_ROWS = 24
-STEPS = 3
-STEP_AUX = AUX // STEPS
-STEP_ROWS = STEP_AUX * ROWS
+HALF = 16
 GAMMA_STEPS = 6
 METRIC_ORDER = ((6, 4, 2), (7, 5, 3, 1))
 
@@ -48,7 +46,7 @@
 def exchange_kernel(
     integrals, coef_t, screening, metric,
     fitted_out, coef_out, mask_out,
-    ints, coef, coef_n, values, mets, scr, pieces, spread, parts, sends, recv1, half, halves, mrecv, columns, rows, mexp, fsend, recv3, fit, pick, lanes, fold,
+    ints, coef, coef_n, mets, scr, pieces, spread, sends, kept, recv1, half, halves, mrecv, columns, rows, mexp, fsend, recv3, fit, pick, lanes, fold,
     load_sem, coef_send, coef_recv, msend, mrecv_sem, fsend_sem, send1, recv1_sem, send2, recv2_sem, send3, recv3_sem,
 ):
     aux = lax.axis_index("aux")
@@ -74,10 +72,10 @@
         pltpu.make_async_copy(screening, scr, load_sem.at[0]),
         pltpu.make_async_copy(coef_t, coef, load_sem.at[1]),
     ]
-    for j in range(STEPS):
-        part = pl.ds(j * STEP_AUX, STEP_AUX)
-        loads.append(pltpu.make_async_copy(integrals.at[part], ints.at[part], load_sem.at[2 + j]))
-    loads.append(pltpu.make_async_copy(metric, mets, load_sem.at[2 + STEPS]))
+    for j in range(2):
+        other_half = pl.ds(pl.multiple_of(lax.rem(xl + 1 + j, 2) * HALF, HALF), HALF)
+        loads.append(pltpu.make_async_copy(integrals.at[:, other_half], ints.at[j], load_sem.at[2 + j]))
+    loads.append(pltpu.make_async_copy(metric, mets, load_sem.at[4]))
     for copy in loads[:2] + loads[-1:] + loads[2:-1]:
         copy.start()
 
@@ -92,18 +90,20 @@
         pl.semaphore_signal(barrier, inc=1, device_id=at_z(-sign * d), device_id_type=MESH)
 
     widen = one_hot(iota((OCC, CHUNKS * LANES), 0) == iota((OCC, CHUNKS * LANES), 1) % OCC)
-    keep = (iota((ROWS, CHUNKS * LANES), 0) % MU) == (iota((ROWS, CHUNKS * LANES), 1) // OCC)
+    keep = (iota((HALF, CHUNKS * LANES), 0) % MU) == (iota((HALF, CHUNKS * LANES), 1) // OCC)
     keep = jnp.tile(jnp.where(keep, 1.0, 0.0).astype(F32), (AUX, 1))
-    row = iota((4 * R, 1), 0)
-    col = iota((1, AUX * ROWS), 1) // MU
+    row = iota((2 * R, 1), 0)
+    col = iota((1, AUX * HALF), 1) // MU
     for c in range(CHUNKS):
         p = row % R - AUX * c
-        wanted = jnp.where((p >= 0) & (p < AUX), p * 4 + row // R, -1)
-        spread[:, c * AUX * ROWS:(c + 1) * AUX * ROWS] = one_hot(wanted == col)
+        wanted = jnp.where((p >= 0) & (p < AUX), p * 2 + row // R, -1)
+        spread[:, c * AUX * HALF:(c + 1) * AUX * HALF] = one_hot(wanted == col)
+    turned = lax.rem(iota((ROWS, ROWS), 0) + (xl + 1) * HALF, ROWS)
+    turned = one_hot(turned == iota((ROWS, ROWS), 1))
     own_tile = one_hot(iota((48, NU), 0) == occ * (NU // TILE) + iota((48, NU), 1) // TILE)
     loads[0].wait()
     screen = scr[...].astype(F32).astype(BF)
-    mask = nn(screen, own_tile).astype(BF)
+    mask = nn(nn(turned, screen).astype(BF), own_tile).astype(BF)
 
     loads[-1].wait()
     pieces[...] = jnp.zeros_like(pieces)
@@ -111,27 +111,28 @@
         pieces[k, 0:AUX, 0:PIECE] = mets[:, k * PIECE:(k + 1) * PIECE]
     mrecv[0] = pieces[z // 2]
 
+    def transform(j):
+        loads[2 + j].wait()
+        block = ints[j] * mask[j * HALF:(j + 1) * HALF][None]
+        value = nn(block.reshape(AUX * HALF, NU), coef_n[...]).astype(BF)
+        wide = (nn(value, widen) * keep).astype(BF)
+        stacked = jnp.concatenate([wide[:, c * LANES:(c + 1) * LANES] for c in range(CHUNKS)], axis=0)
+        return nn(spread[...], stacked).reshape(2, R, LANES)
+
+    def send_partial(k):
+        copy = pltpu.make_async_remote_copy(
+            src_ref=sends.at[1 - k // 2, lax.rem(core + k % 2, 2)], dst_ref=recv1.at[k - 1],
+            send_sem=send1.at[k - 1], recv_sem=recv1_sem.at[k - 1],
+            device_id={"aux": aux, "occ": mate(k)}, device_id_type=MESH)
+        copy.start()
+        return copy
+
     loads[1].wait()
     coef_n[...] = coef[...].T
-    for j in range(STEPS):
-        loads[2 + j].wait()
-        block = ints[j * STEP_AUX:(j + 1) * STEP_AUX] * mask[None]
-        values[j * STEP_ROWS:(j + 1) * STEP_ROWS, :] = nn(block.reshape(STEP_ROWS, NU), coef_n[...]).astype(BF)
-    wide = (nn(values[...], widen) * keep).astype(BF)
-    for c in range(CHUNKS):
-        parts[c * AUX * ROWS:(c + 1) * AUX * ROWS, :] = wide[:, c * LANES:(c + 1) * LANES]
-    sends[...] = nn(spread[...], parts[...]).astype(BF).reshape(4, R, LANES)
-
+    sends[0] = transform(0).astype(BF)
     pl.semaphore_wait(barrier, 28)
 
-    first = []
-    for k in (3, 2, 1):
-        copy = pltpu.make_async_remote_copy(
-            src_ref=sends.at[mate(k)], dst_ref=recv1.at[k - 1], send_sem=send1.at[k - 1], recv_sem=recv1_sem.at[k - 1],
-            device_id={"aux": aux, "occ": mate(k)}, device_id_type=MESH)
-        copy.start()
-        first.append(copy)
-
+    first = [send_partial(3), send_partial(2)]
     def metric_copy(d):
         step = sign * d if d % 2 else -sign * d
         other = lax.rem(z + step + 16, 16)
@@ -149,9 +150,14 @@
         def _():
             for d in METRIC_ORDER[turn]:
                 metric_copy(d).start()
-    for copy in first:
+    own = transform(1)
+    sends[1] = own.astype(BF)
+    first.append(send_partial(1))
+    kept[...] = own
+    total = kept[core]
+    for copy, k in zip(first[::-1], (1, 2, 3)):
         copy.wait_recv()
-    total = sends[occ].astype(F32) + recv1[0].astype(F32) + recv1[1].astype(F32) + recv1[2].astype(F32)
+        total = total + recv1[k - 1].astype(F32)
     half[...] = total.astype(BF)
 
     second = []
@@ -207,17 +213,21 @@
 
     for copy in second:
         copy.wait_recv()
-    partial = nn(mexp[...], halves[...].reshape(16 * R, LANES)).reshape(8, R, LANES)
-    fsend[...] = partial.astype(BF)
-
+    gathered = halves[...].reshape(16 * R, LANES)
     third = []
-    for d in (7, 6, 5, 4, 3, 2, 1):
-        copy = pltpu.make_async_remote_copy(
-            src_ref=fsend.at[d], dst_ref=recv3.at[d - 1], send_sem=send3.at[d - 1], recv_sem=recv3_sem.at[d - 1],
-            device_id=at_z(sign * d), device_id_type=MESH)
-        copy.start()
-        third.append(copy)
-    fit[...] = partial[0]
+    for part in ((7, 6, 5, 4), (3, 2, 1, 0)):
+        partial = nn(mexp[part[-1] * R:(part[0] + 1) * R, :], gathered)
+        for d in part:
+            lo = (d - part[-1]) * R
+            if d == 0:
+                fit[...] = partial[lo:lo + R]
+                continue
+            fsend[d] = partial[lo:lo + R].astype(BF)
+            copy = pltpu.make_async_remote_copy(
+                src_ref=fsend.at[d], dst_ref=recv3.at[d - 1], send_sem=send3.at[d - 1], recv_sem=recv3_sem.at[d - 1],
+                device_id=at_z(sign * d), device_id_type=MESH)
+            copy.start()
+            third.append(copy)
 
     to_chip.wait_recv()
     chip_nu = pl.ds(pl.multiple_of(mate(2) * NU, NU), NU)
@@ -278,16 +288,15 @@
         in_specs=[hbm, hbm, hbm, hbm],
         out_specs=(vmem, free, vmem),
         scratch_shapes=[
-            pltpu.VMEM((AUX, ROWS, NU), BF),
+            pltpu.VMEM((2, AUX, HALF, NU), BF),
             pltpu.VMEM((OCC, NU), BF),
             pltpu.VMEM((NU, OCC), BF),
-            pltpu.VMEM((AUX * ROWS, OCC), BF),
             pltpu.VMEM((AUX, 2304), BF),
             pltpu.VMEM((ROWS, 48), jnp.int32),
             pltpu.VMEM((8, PIECE_ROWS, PIECE_PAD), BF),
-            pltpu.VMEM((4 * R, CHUNKS * AUX * ROWS), BF),
-            pltpu.VMEM((CHUNKS * AUX * ROWS, LANES), BF),
-            pltpu.VMEM((4, R, LANES), BF),
+            pltpu.VMEM((2 * R, CHUNKS * AUX * HALF), BF),
+            pltpu.VMEM((2, 2, R, LANES), BF),
+            pltpu.VMEM((2, R, LANES), F32),
             pltpu.VMEM((3, R, LANES), BF),
             pltpu.VMEM((R, LANES), BF),
             pltpu.VMEM((16, R, LANES), BF),
@@ -301,7 +310,7 @@
             pltpu.VMEM((CHUNKS * AUX * MU, R), BF),
             pltpu.VMEM((CHUNKS * AUX * MU, LANES), F32),
             pltpu.VMEM((CHUNKS * LANES, OCC), BF),
-            dma((STEPS + 3,)),
+            dma((5,)),
             dma((3,)), dma((3,)),
             dma((7,)), dma((7,)), dma((7,)),
             dma((3,)), dma((3,)),

time: 34.5 us -> 34.3 us (level)
  no operation moved by 1% of the time
where the time goes in v4:
time: 34.3 us; the launch traced here: 34.1 us
  Pallas kernels  34 us (99%)
    pallas_call x1, Pallas kernels, on_device(): pl.pallas_call(exchange_kernel, name='exchange', out_shape=(jax.ShapeDtyp...  32.6 us
    pallas_call x1, Pallas kernels, on_device(): pl.pallas_call(gamma_kernel, name='gamma', out_shape=jax.ShapeDtypeStruct...  1.47 us

profile of v4, /device:TPU:8, one launch (start us, length us, event | category | flops | bytes accessed | tf_op | source)
XLA Modules:
  0.0 34.1 jit_solution(16022199940291117563)
XLA Ops:
  0.0 32.6 %exchange.1 = (bf16[144,48]{1,0:T(8,128)(2,1)S(1)}, bf16[48,6144]{1,0:T(8,128)(2,1)S(1)}, f32[8,6144]{1,0:T(8,128)S(1)}) custom-call(bf16[18,32,1536]{2,1,0:T(8,128)(2,1)} %integrals.1, bf16[48,1536]{1,0:T(8,128)(2,1)} %bitcast.2, s32[32,48]{1,0:T(8,128)} %screening.1, bf16[18,2304]{1,0:T(8,128)(2,1)} %metric.1), custom_call_target="tpu_custom_call" | custom-call | tf_op jit(solution)/shard_map/exchange/pallas_call | solution.py:280
  32.6 1.5 %gamma.1 = bf16[144,6144]{1,0:T(8,128)(2,1)} custom-call(bf16[144,48]{1,0:T(8,128)(2,1)S(1)} %get-tuple-element.8.fitted, bf16[48,6144]{1,0:T(8,128)(2,1)S(1)} %get-tuple-element.9.coef, f32[8,6144]{1,0:T(8,128)S(1)} %get-tuple-element.10.mask), custom_call_target="tpu_custom_call" | custom-call | tf_op jit(solution)/shard_map/gamma/pallas_call | solution.py:322

commit v5 on v4

--- a/solution.py
+++ b/solution.py
@@ -24,7 +24,7 @@
 PIECE_ROWS = 24
 HALF = 16
 GAMMA_STEPS = 6
-METRIC_ORDER = ((6, 4, 2), (7, 5, 3, 1))
+METRIC_ORDER = ((7, 4, 3), (6, 5, 2, 1))
 
 
 def iota(shape, dim):

time: 34.3 us -> 34.7 us (1.012)
  the two profiles are of different devices: /device:TPU:8 before, /device:TPU:2 now
where the time goes in v5:
time: 34.7 us; the launch traced here: 34.5 us
  Pallas kernels  34.5 us (99%)
    pallas_call x1, Pallas kernels, on_device(): pl.pallas_call(exchange_kernel, name='exchange', out_shape=(jax.ShapeDtyp...  33 us
    pallas_call x1, Pallas kernels, on_device(): pl.pallas_call(gamma_kernel, name='gamma', out_shape=jax.ShapeDtypeStruct...  1.47 us

profile of v5, /device:TPU:2, one launch (start us, length us, event | category | flops | bytes accessed | tf_op | source)
XLA Modules:
  0.0 34.5 jit_solution(4617883222076675378)
XLA Ops:
  0.0 33.0 %exchange.1 = (bf16[144,48]{1,0:T(8,128)(2,1)S(1)}, bf16[48,6144]{1,0:T(8,128)(2,1)S(1)}, f32[8,6144]{1,0:T(8,128)S(1)}) custom-call(bf16[18,32,1536]{2,1,0:T(8,128)(2,1)} %integrals.1, bf16[48,1536]{1,0:T(8,128)(2,1)} %bitcast.2, s32[32,48]{1,0:T(8,128)} %screening.1, bf16[18,2304]{1,0:T(8,128)(2,1)} %metric.1), custom_call_target="tpu_custom_call" | custom-call | tf_op jit(solution)/shard_map/exchange/pallas_call | solution.py:280
  33.0 1.5 %gamma.1 = bf16[144,6144]{1,0:T(8,128)(2,1)} custom-call(bf16[144,48]{1,0:T(8,128)(2,1)S(1)} %get-tuple-element.8.fitted, bf16[48,6144]{1,0:T(8,128)(2,1)S(1)} %get-tuple-element.9.coef, f32[8,6144]{1,0:T(8,128)S(1)} %get-tuple-element.10.mask), custom_call_target="tpu_custom_call" | custom-call | tf_op jit(solution)/shard_map/gamma/pallas_call | solution.py:322
